TPU v7x, 32 devices: a whole 2x2x4 slice. The times are simulated.
32 devices in a mesh: dp: 8 (over y, x, core), ctx: 4 (over z).
Axes of the slice: x: 2, y: 2, z: 4, core: 2. Of those that a mesh axis runs over, the one named last changes fastest.
Arguments:
- normed: bfloat16 [8, 512, 5376], P('dp', 'ctx'), may hold values from -6 to 6
- queries: bfloat16 [8, 512, 2048], P('dp', 'ctx'), may hold values from -8 to 8
- keys: bfloat16 [8, 512, 1024], P('dp', 'ctx'), may hold values from -8 to 8
- values: bfloat16 [8, 512, 1024], P('dp', 'ctx'), may hold values from -6 to 6
- out_grad: bfloat16 [8, 512, 2048], P('dp', 'ctx'), may hold values from -150 to 150
- segment_ids: int32 [8, 512], P('dp'), may hold values from 0 to 3, never falling along the last dimension, each value on 1 to 384 neighbouring positions
Outputs:
- grad_queries: bfloat16 [8, 512, 2048], P('dp', 'ctx')
- grad_keys: bfloat16 [8, 512, 1024], P('dp', 'ctx')
- grad_values: bfloat16 [8, 512, 1024], P('dp', 'ctx')
- grad_weight: bfloat16 [5376, 1024], P('ctx', 'dp')
Inputs may be any that keep to these rules, and one draw needn't show every extreme that they name: `segment_ids`: within a sequence the document numbers never fall, and a document has at most 384 positions.
All inputs are finite; a program needn't handle non-finite values.
Results may differ from a plain program's by a relative error of at most 0.022.
Values may be sent and summed in bfloat16 or wider, within the bound.
A program may use at most 128 MiB of HBM per device.

v0:
```python
import jax
import jax.numpy as jnp
from jax import lax
from jax.sharding import PartitionSpec as P

HEAD_SIZE = 128
WINDOW = 1024


query_scalar = 168.0


def passed_along(shard, axis, by):
    size = lax.axis_size(axis)
    pairs = [(i, i + by) for i in range(size) if 0 <= i + by < size]
    return lax.ppermute(shard, axis, pairs)


def band_core(queries, keys, values, out_grad, allowed):
    count = queries.shape[0]
    span = keys.shape[0]
    groups = keys.shape[1] // HEAD_SIZE
    ratio = queries.shape[1] // keys.shape[1]
    softmax_scale = query_scalar ** (-0.5)
    query_head_rows = queries.reshape(count, groups, ratio, HEAD_SIZE)
    key_head_rows = keys.reshape(span, groups, HEAD_SIZE)
    value_head_rows = values.reshape(span, groups, HEAD_SIZE)
    head_gradient = out_grad.reshape(count, groups, ratio, HEAD_SIZE)
    attention_scores = (
        jnp.einsum(
            "qczw,jcw->czqj", query_head_rows, key_head_rows, preferred_element_type=jnp.float32
        )
        * softmax_scale
    )
    attention_scores = jnp.where(allowed[None, None], attention_scores, -jnp.inf)
    highest = jnp.max(attention_scores, axis=-1, keepdims=True)
    expanded = jnp.exp(attention_scores - highest)
    weights_full = expanded / jnp.sum(expanded, axis=-1, keepdims=True)
    reduced_precision_weight = weights_full.astype(jnp.bfloat16)
    attention_output = jnp.einsum(
        "mlhv,vmo->mlho",
        reduced_precision_weight,
        value_head_rows,
        preferred_element_type=jnp.float32,
    )
    grad_major = jnp.transpose(head_gradient, (1, 2, 0, 3)).astype(jnp.float32)
    delta = jnp.sum(grad_major * attention_output, axis=-1, keepdims=True)
    probability_gradient = jnp.einsum(
        "qczw,jcw->czqj", head_gradient, value_head_rows, preferred_element_type=jnp.float32
    )
    score_gradient = (weights_full * (probability_gradient - delta)).astype(jnp.bfloat16)
    query_gradient = (
        jnp.einsum(
            "fwcj,jfe->cfwe", score_gradient, key_head_rows, preferred_element_type=jnp.float32
        )
        * softmax_scale
    )
    key_gradient = (
        jnp.einsum(
            "vbzp,zvba->pva", score_gradient, query_head_rows, preferred_element_type=jnp.float32
        )
        * softmax_scale
    )
    value_gradient = jnp.einsum(
        "vbzp,zvba->pva",
        reduced_precision_weight,
        head_gradient,
        preferred_element_type=jnp.float32,
    )
    return (
        query_gradient.reshape(count, -1).astype(jnp.bfloat16),
        key_gradient.reshape(span, -1).astype(jnp.bfloat16),
        value_gradient.reshape(span, -1).astype(jnp.bfloat16),
    )


def band_heads(queries, keys, values, out_grad, allowed):
    groups = keys.shape[1] // HEAD_SIZE
    ratio = queries.shape[1] // keys.shape[1]
    portion = max(1, groups // 2)
    query_parts = []
    key_parts = []
    value_parts = []
    for lowest in range(0, groups, portion):
        upper = min(groups, lowest + portion)
        query_lo = lowest * ratio * HEAD_SIZE
        query_hi = upper * ratio * HEAD_SIZE
        key_lo = lowest * HEAD_SIZE
        key_hi = upper * HEAD_SIZE
        query_gradient, key_gradient, value_gradient = band_core(
            queries[:, query_lo:query_hi],
            keys[:, key_lo:key_hi],
            values[:, key_lo:key_hi],
            out_grad[:, query_lo:query_hi],
            allowed,
        )
        query_parts.append(query_gradient)
        key_parts.append(key_gradient)
        value_parts.append(value_gradient)
    return (
        jnp.concatenate(query_parts, axis=1),
        jnp.concatenate(key_parts, axis=1),
        jnp.concatenate(value_parts, axis=1),
    )


def body(normed, queries, keys, values, out_grad, segment_ids):
    count = queries.shape[1]
    width = keys.shape[2]
    window = WINDOW
    spans = window // count
    chain = lax.axis_size("ctx")
    place = lax.axis_index("ctx")
    start = place * count
    pairs = (keys, values)
    pieces = []
    for back in range(spans, 0, -1):
        if back < chain:
            pieces.append(passed_along((pairs[0], pairs[1]), "ctx", back))
        else:
            pieces.append((jnp.zeros_like(keys), jnp.zeros_like(values)))
    near_keys = jnp.concatenate([piece[0] for piece in pieces] + [keys], axis=1)
    near_values = jnp.concatenate([piece[1] for piece in pieces] + [values], axis=1)
    padded_ids = jnp.concatenate([jnp.full((1, window), -1, jnp.int32), segment_ids], axis=1)
    key_ids = lax.dynamic_slice_in_dim(padded_ids, start, window + count, 1)[0]
    query_ids = lax.dynamic_slice_in_dim(segment_ids, start, count, 1)[0]
    offsets = (
        jnp.arange(count, dtype=jnp.int32)[:, None]
        - jnp.arange(window + count, dtype=jnp.int32)[None, :]
        + window
    )
    allowed = (query_ids[:, None] == key_ids[None, :]) & (offsets >= 0) & (offsets < window)
    query_gradient, key_part, value_part = band_heads(
        queries[0], near_keys[0], near_values[0], out_grad[0], allowed
    )
    own_key = key_part[window:].astype(jnp.float32)
    own_value = value_part[window:].astype(jnp.float32)
    for back in range(1, spans + 1):
        if back < chain:
            lower = window - back * count
            got_key, got_value = passed_along(
                (key_part[None, lower : lower + count], value_part[None, lower : lower + count]),
                "ctx",
                -back,
            )
            own_key = own_key + got_key[0].astype(jnp.float32)
            own_value = own_value + got_value[0].astype(jnp.float32)
    key_gradient = own_key.astype(jnp.bfloat16)[None]
    value_gradient = own_value.astype(jnp.bfloat16)[None]
    features = normed.shape[2]
    columns = lax.all_to_all(normed, "ctx", split_axis=2, concat_axis=1, tiled=True)[0]
    initial = jnp.zeros((features // chain, width), jnp.float32)
    piece = lax.all_gather(value_gradient, "ctx", axis=1, tiled=True)
    shards = piece.shape[1] // count

    def one_shard(index, running):
        rows_here = lax.dynamic_slice_in_dim(piece[0], index * count, count, 0)
        feature_rows = lax.dynamic_slice_in_dim(columns, index * count, count, 0)
        term = jnp.einsum("td,tf->df", feature_rows, rows_here, preferred_element_type=jnp.float32)
        return running + term.astype(jnp.bfloat16).astype(jnp.float32)

    token_sum = lax.fori_loop(0, shards, one_shard, initial)
    sequence_sum = lax.psum_scatter(
        token_sum.astype(jnp.bfloat16), "dp", scatter_dimension=1, tiled=True
    ).astype(jnp.float32)
    total_tokens = count * chain * lax.axis_size("dp")
    grad_weight = (sequence_sum * total_tokens ** (-0.5)).astype(jnp.bfloat16)
    return (query_gradient[None], key_gradient, value_gradient, grad_weight)


def solution(mesh):
    placed = (
        P("dp", "ctx", None),
        P("dp", "ctx", None),
        P("dp", "ctx", None),
        P("dp", "ctx", None),
        P("dp", "ctx", None),
        P("dp", None),
    )
    return jax.shard_map(
        body,
        mesh=mesh,
        in_specs=placed,
        out_specs=(
            P("dp", "ctx", None),
            P("dp", "ctx", None),
            P("dp", "ctx", None),
            P("ctx", "dp"),
        ),
        check_vma=False,
    )
```

profile of v0, /device:TPU:0, one launch (start us, length us, event | category | flops | bytes accessed | tf_op | source)
XLA Modules:
  0.0 288.1 jit_solution(10406556506468076428)
XLA Ops:
  7.2 1.2 copy.102
  8.4 5.0 %collective-permute-start.2 = (bf16[1,128,1024]{1,2,0:T(8,128)(2,1)S(1)}, bf16[1,128,1024]{1,2,0:T(8,128)(2,1)S(1)}, u32[]{:S(2)}, u32[]{:S(2)}) collective-permute-start(bf16[1,128,1024]{1,2,0:T(8,128)(2,1)S(1)} %copy.102), channel_id=1, source_target_pairs={{0,1},{1,2},{2,3},{4,5},{5,6},{6,7},{8,9},{9,10},{10,11},{12,13},{... | collective-permute-start | bytes 786440 | tf_op jit(solution)/shard_map/ppermute | solution.py:16
  13.3 4.5 %collective-permute-start.1 = (bf16[1,128,1024]{1,2,0:T(8,128)(2,1)S(1)}, bf16[1,128,1024]{1,2,0:T(8,128)(2,1)S(1)}, u32[]{:S(2)}, u32[]{:S(2)}) collective-permute-start(bf16[1,128,1024]{1,2,0:T(8,128)(2,1)S(1)} %copy.102), channel_id=1, source_target_pairs={{0,2},{1,3},{4,6},{5,7},{8,10},{9,11},{12,14},{13,15},{16,18},{17,... | collective-permute-start | bytes 786440 | tf_op jit(solution)/shard_map/ppermute | solution.py:16
  17.8 1.3 collective-permute-start
  20.5 1.3 copy.106
  23.9 6.2 %collective-permute-done = bf16[1,128,1024]{1,2,0:T(8,128)(2,1)S(1)} collective-permute-done((bf16[1,128,1024]{1,2,0:T(8,128)(2,1)S(1)}, bf16[1,128,1024]{1,2,0:T(8,128)(2,1)S(1)}, u32[]{:S(2)}, u32[]{:S(2)}) %collective-permute-start) | collective-permute-done | bytes 262176 | tf_op jit(solution)/shard_map/ppermute | solution.py:16
  30.5 1.3 fusion.45
  31.7 3.9 %exponential_reduce_fusion = (f32[4,2,128]{2,1,0:T(2,128)S(1)}, f32[4,2,128,1152]{2,3,1,0:T(8,128)}) fusion(pred[128,1152]{0,1:T(8,128)(4,1)S(1)} %fusion.33, bf16[1152,4,128,1]{0,2,3,1:T(8,128)(2,1)S(1)} %bitcast.192, bf16[128,4,2,128]{0,3,2,1:T(8,128)(2,1)S(1)} %bitcast.221), kind=kOutput, calls=%fused_computation.23 | convolution fusion | flops 306709632 | bytes 6311936 | tf_op jit(solution)/shard_map/sub | solution.py:37
  35.6 3.0 %fusion.25 = bf16[4,2,128,1152]{2,3,1,0:T(8,128)(2,1)S(1)} fusion(f32[4,2,128]{2,1,0:T(2,128)S(1)} %get-tuple-element.121, f32[4,2,128,1152]{2,3,1,0:T(8,128)} %get-tuple-element.122), kind=kLoop, calls=%fused_computation.41 | loop fusion | flops 2359296 | bytes 7081984 | tf_op jit(solution)/shard_map/convert_element_type | solution.py:39
  38.6 1.4 copy-done
  39.9 1.9 fusion.19
  41.8 1.7 copy.133
  43.5 3.8 %exponential_reduce_fusion.1 = (f32[4,2,128]{2,1,0:T(2,128)S(1)}, f32[4,2,128,1152]{2,3,1,0:T(8,128)}) fusion(pred[128,1152]{0,1:T(8,128)(4,1)S(1)} %copy-done.23, bf16[1152,4,128,1]{0,2,3,1:T(8,128)(2,1)S(1)} %bitcast.190, bf16[128,4,2,128]{0,3,2,1:T(8,128)(2,1)S(1)} %bitcast.219), kind=kOutput, calls=%fused_computation.25 | convolution fusion | flops 306709632 | bytes 6311936 | tf_op jit(solution)/shard_map/sub | solution.py:37
  47.4 3.0 %fusion.24 = bf16[4,2,128,1152]{2,3,1,0:T(8,128)(2,1)S(1)} fusion(f32[4,2,128]{2,1,0:T(2,128)S(1)} %get-tuple-element.123, f32[4,2,128,1152]{2,3,1,0:T(8,128)} %get-tuple-element.124), kind=kLoop, calls=%fused_computation.40 | loop fusion | flops 2359296 | bytes 7081984 | tf_op jit(solution)/shard_map/convert_element_type | solution.py:39
  50.4 1.9 fusion.18
  52.3 2.4 copy.132
  54.7 2.0 maximum_bitcast_fusion.2
  56.6 1.3 collective-permute-start.9
  57.9 1.3 collective-permute-start.10
  59.2 1.5 collective-permute-start.11
  60.7 6.8 %copy.134 = bf16[1,128,5376]{1,0,2:T(2,128)(2,1)} copy(bf16[1,128,5376]{2,1,0:T(8,128)(2,1)} %param.8) | data formatting | bytes 2752512 | tf_op args[0]
  68.1 31.3 %reduce.2 = bf16[5376,128]{1,0:T(8,128)(2,1)} reduce(bf16[5376,1,128]{2,1,0:T(2,128)(2,1)} %bitcast.188, bf16[]{:T(256)} %broadcast.111), dimensions={1}, to_apply=%bitcast.155.reduce_sub_computation | reduce | bytes 2752514
  99.3 3.7 %reshape.143 = bf16[4,2,86016]{2,1,0:T(2,128)(2,1)} reshape(bf16[5376,128]{1,0:T(8,128)(2,1)} %reduce.2) | data formatting | bytes 2752512
  103.0 13.1 %all-to-all-start = ((bf16[4,2,86016]{2,1,0:T(2,128)(2,1)}), bf16[4,2,86016]{2,1,0:T(2,128)(2,1)}, u32[]{:S(2)}, u32[]{:S(2)}) async-start(bf16[4,2,86016]{2,1,0:T(2,128)(2,1)} %reshape.143), calls=%async_computation | async-start | bytes 2752512 | tf_op jit(solution)/shard_map/all_to_all | solution.py:151
  116.2 2.0 fusion.34
  118.3 1.1 copy.109
  119.4 5.7 %collective-permute-start.3 = (bf16[1,128,1024]{1,2,0:T(8,128)(2,1)S(1)}, bf16[1,128,1024]{1,2,0:T(8,128)(2,1)S(1)}, u32[]{:S(2)}, u32[]{:S(2)}) collective-permute-start(bf16[1,128,1024]{1,2,0:T(8,128)(2,1)S(1)} %copy.109), channel_id=1, source_target_pairs={{0,3},{4,7},{8,11},{12,15},{16,19},{20,23},{24,27},{28,31}} | collective-permute-start | bytes 786440 | tf_op jit(solution)/shard_map/ppermute | solution.py:16
  125.2 1.3 collective-permute-start.5
  126.5 2.7 collective-permute-start.4
  129.9 1.1 broadcast_dynamic-update-slice_fusion
  130.9 30.9 %collective-permute-done.3 = bf16[1,128,1024]{1,2,0:T(8,128)(2,1)S(1)} collective-permute-done((bf16[1,128,1024]{1,2,0:T(8,128)(2,1)S(1)}, bf16[1,128,1024]{1,2,0:T(8,128)(2,1)S(1)}, u32[]{:S(2)}, u32[]{:S(2)}) %collective-permute-start.3) | collective-permute-done | bytes 262176 | tf_op jit(solution)/shard_map/ppermute | solution.py:16
  162.6 8.7 %collective-permute-done.4 = bf16[1,128,1024]{1,2,0:T(8,128)(2,1)S(1)} collective-permute-done((bf16[1,128,1024]{1,2,0:T(8,128)(2,1)S(1)}, bf16[1,128,1024]{1,2,0:T(8,128)(2,1)S(1)}, u32[]{:S(2)}, u32[]{:S(2)}) %collective-permute-start.4) | collective-permute-done | bytes 262176 | tf_op jit(solution)/shard_map/ppermute | solution.py:16
  171.3 0.8 constant_dynamic-update-slice_fusion.6
  172.8 0.8 constant_dynamic-update-slice_fusion.4
  173.6 4.3 %reshape.144 = bf16[5376,1,128]{2,1,0:T(2,128)(2,1)} reshape(bf16[4,2,86016]{2,1,0:T(2,128)(2,1)} %all-to-all-done) | data formatting | bytes 2752512
  177.9 3.0 %copy.170 = bf16[1,128,5376]{1,2,0:T(8,128)(2,1)} copy(bf16[1,128,5376]{1,0,2:T(2,128)(2,1)} %bitcast.189) | data formatting | bytes 2752512
  180.9 2.5 copy.135
  183.5 22.6 %while.14 = (s32[]{:T(128)}, f32[1344,1024]{1,0:T(8,128)}, bf16[512,1344]{1,0:T(8,128)(2,1)}, bf16[1,512,1024]{2,1,0:T(8,128)(2,1)}, s32[]{:T(128)}, /*index=5*/s32[]{:T(128)}, s32[]{:T(128)}, s32[]{:T(128)}) while((s32[]{:T(128)}, f32[1344,1024]{1,0:T(8,128)}, bf16[512,1344]{1,0:T(8,128)(2,1)}, bf16[1,512,1024]{2,1,0:T(8,128)(2,1)}, ...), condition=%wide.region_7.8_spmd.clone, body=%wide.region_6.7_spmd.clone.sunk | while | flops 357826560 | bytes 11634324 | solution.py:162
  183.5 4.4 %select_add_fusion.2 = f32[1344,1024]{1,0:T(8,128)} fusion(f32[1344,1024]{1,0:T(8,128)} %get-tuple-element.159, pred[]{:T(512)S(6)} %compare.4, bf16[512,1344]{1,0:T(8,128)(2,1)} %get-tuple-element.168, s32[]{:T(128)S(6)} %select_n.39, bf16[1,512,1024]{2,1,0:T(8,128)(2,1)} %get-tuple-element.169), kind=kOutput, calls=%fused_computation.clone.1 | convolution fusion | flops 357826560 | bytes 11634176 | tf_op jit(solution)/shard_map/while/body/eval_jaxpr/td,tf->df/dot_general | solution.py:159
  187.8 6.1 %select_add_fusion.2 = f32[1344,1024]{1,0:T(8,128)} fusion(f32[1344,1024]{1,0:T(8,128)} %get-tuple-element.159, pred[]{:T(512)S(6)} %compare.4, bf16[512,1344]{1,0:T(8,128)(2,1)} %get-tuple-element.168, s32[]{:T(128)S(6)} %select_n.39, bf16[1,512,1024]{2,1,0:T(8,128)(2,1)} %get-tuple-element.169), kind=kOutput, calls=%fused_computation.clone.1 | convolution fusion | flops 357826560 | bytes 11634176 | tf_op jit(solution)/shard_map/while/body/eval_jaxpr/td,tf->df/dot_general | solution.py:159
  193.9 6.1 %select_add_fusion.2 = f32[1344,1024]{1,0:T(8,128)} fusion(f32[1344,1024]{1,0:T(8,128)} %get-tuple-element.159, pred[]{:T(512)S(6)} %compare.4, bf16[512,1344]{1,0:T(8,128)(2,1)} %get-tuple-element.168, s32[]{:T(128)S(6)} %select_n.39, bf16[1,512,1024]{2,1,0:T(8,128)(2,1)} %get-tuple-element.169), kind=kOutput, calls=%fused_computation.clone.1 | convolution fusion | flops 357826560 | bytes 11634176 | tf_op jit(solution)/shard_map/while/body/eval_jaxpr/td,tf->df/dot_general | solution.py:159
  200.0 6.1 %select_add_fusion.2 = f32[1344,1024]{1,0:T(8,128)} fusion(f32[1344,1024]{1,0:T(8,128)} %get-tuple-element.159, pred[]{:T(512)S(6)} %compare.4, bf16[512,1344]{1,0:T(8,128)(2,1)} %get-tuple-element.168, s32[]{:T(128)S(6)} %select_n.39, bf16[1,512,1024]{2,1,0:T(8,128)(2,1)} %get-tuple-element.169), kind=kOutput, calls=%fused_computation.clone.1 | convolution fusion | flops 357826560 | bytes 11634176 | tf_op jit(solution)/shard_map/while/body/eval_jaxpr/td,tf->df/dot_general | solution.py:159
  206.1 4.5 %convert_element_type.191 = bf16[1344,1024]{1,0:T(8,128)(2,1)} convert(f32[1344,1024]{1,0:T(8,128)} %get-tuple-element.83) | non-fusion elementwise | flops 1376256 | bytes 8257536 | tf_op jit(solution)/shard_map/convert_element_type | solution.py:164
  210.6 4.5 %copy.168 = bf16[1344,1024]{0,1:T(8,128)(2,1)} copy(bf16[1344,1024]{1,0:T(8,128)(2,1)} %convert_element_type.191) | data formatting | bytes 5505024
  215.2 3.0 %fusion.44 = (bf16[1152,512]{0,1:T(8,128)(2,1)}, bf16[1152,512]{0,1:T(8,128)(2,1)S(1)}) fusion(bf16[1152,1024]{0,1:T(8,128)(2,1)} %bitcast.9), kind=kLoop, calls=%fused_computation.93 | loop fusion | bytes 4718592 | tf_op jit(solution)/shard_map/slice | solution.py:93
  219.4 1.2 fusion.9
  220.7 1.5 copy-done.2
  222.2 1.9 fusion.17
  224.0 1.6 copy.129
  225.6 2.0 fusion.28
  227.6 3.6 %fusion.11 = bf16[4,2,128,1152]{2,3,1,0:T(8,128)(2,1)S(1)} fusion(bf16[1152,4,128,1]{0,2,3,1:T(8,128)(2,1)S(1)} %bitcast.195, bf16[128,4,2,128]{0,3,2,1:T(8,128)(2,1)S(1)} %bitcast.208, f32[4,2,128]{2,1,0:T(2,128)S(1)} %fusion.28, f32[4,2,128]{2,1,0:T(2,128)S(1)} %get-tuple-element.123, f32[4,2,128,1152]{2,3,1,0:T(8,128)} %get-tuple-element.124), kind=kOutput, calls=%fused_computation.18 | convolution fusion | flops 306708480 | bytes 8527872 | tf_op jit(solution)/shard_map/qczw,jcw->czqj/dot_general | solution.py:48
  231.3 1.9 fusion.16
  233.2 2.6 copy.128
  235.8 2.0 maximum_bitcast_fusion.4
  237.8 1.3 collective-permute-start.6
  239.1 1.3 collective-permute-start.7
  240.4 1.6 collective-permute-start.8
  242.0 1.3 fusion.27
  244.5 0.8 maximum_bitcast_fusion
  245.4 15.5 %collective-permute-done.6 = bf16[1,128,1024]{2,1,0:T(8,128)(2,1)} collective-permute-done((bf16[1,128,1024]{2,1,0:T(8,128)(2,1)}, bf16[1,128,1024]{2,1,0:T(8,128)(2,1)}, u32[]{:S(2)}, u32[]{:S(2)}) %collective-permute-start.6) | collective-permute-done | bytes 262176 | tf_op jit(solution)/shard_map/ppermute | solution.py:16
  260.8 16.4 %collective-permute-done.7 = bf16[1,128,1024]{2,1,0:T(8,128)(2,1)} collective-permute-done((bf16[1,128,1024]{2,1,0:T(8,128)(2,1)}, bf16[1,128,1024]{2,1,0:T(8,128)(2,1)}, u32[]{:S(2)}, u32[]{:S(2)}) %collective-permute-start.7) | collective-permute-done | bytes 262176 | tf_op jit(solution)/shard_map/ppermute | solution.py:16
  277.3 2.0 fusion.36
  279.2 1.2 copy.169
  280.4 0.8 multiply_convert_fusion
  (86 shorter events, 9.1 us)
Async XLA Ops:
  7.2 15.4 %copy-start.21 = (bf16[1,128,2048]{2,1,0:T(8,128)(2,1)S(1)}, bf16[1,128,2048]{2,1,0:T(8,128)(2,1)}, u32[]{:S(2)}) copy-start(bf16[1,128,2048]{2,1,0:T(8,128)(2,1)} %param.12) | copy-start | bytes 1572868
  8.4 21.9 %collective-permute-start.2 = (bf16[1,128,1024]{1,2,0:T(8,128)(2,1)S(1)}, bf16[1,128,1024]{1,2,0:T(8,128)(2,1)S(1)}, u32[]{:S(2)}, u32[]{:S(2)}) collective-permute-start(bf16[1,128,1024]{1,2,0:T(8,128)(2,1)S(1)} %copy.102), channel_id=1, source_target_pairs={{0,1},{1,2},{2,3},{4,5},{5,6},{6,7},{8,9},{9,10},{10,11},{12,13},{... | collective-permute-start | bytes 786440 | tf_op jit(solution)/shard_map/ppermute | solution.py:16
  13.3 16.9 %collective-permute-start.1 = (bf16[1,128,1024]{1,2,0:T(8,128)(2,1)S(1)}, bf16[1,128,1024]{1,2,0:T(8,128)(2,1)S(1)}, u32[]{:S(2)}, u32[]{:S(2)}) collective-permute-start(bf16[1,128,1024]{1,2,0:T(8,128)(2,1)S(1)} %copy.102), channel_id=1, source_target_pairs={{0,2},{1,3},{4,6},{5,7},{8,10},{9,11},{12,14},{13,15},{16,18},{17,... | collective-permute-start | bytes 786440 | tf_op jit(solution)/shard_map/ppermute | solution.py:16
  17.8 12.3 %collective-permute-start = (bf16[1,128,1024]{1,2,0:T(8,128)(2,1)S(1)}, bf16[1,128,1024]{1,2,0:T(8,128)(2,1)S(1)}, u32[]{:S(2)}, u32[]{:S(2)}) collective-permute-start(bf16[1,128,1024]{1,2,0:T(8,128)(2,1)S(1)} %copy.102), channel_id=1, source_target_pairs={{0,3},{4,7},{8,11},{12,15},{16,19},{20,23},{24,27},{28,31}} | collective-permute-start | bytes 786440 | tf_op jit(solution)/shard_map/ppermute | solution.py:16
  22.6 9.2 %copy-start.19 = (bf16[128,1024]{0,1:T(8,128)(2,1)}, bf16[128,1024]{0,1:T(8,128)(2,1)S(1)}, u32[]{:S(2)}) copy-start(bf16[128,1024]{0,1:T(8,128)(2,1)S(1)} %get-tuple-element.118) | copy-start | bytes 786436
  23.1 8.6 %copy-start.22 = (pred[128,1152]{0,1:T(8,128)(4,1)}, pred[128,1152]{0,1:T(8,128)(4,1)S(1)}, u32[]{:S(2)}) copy-start(pred[128,1152]{0,1:T(8,128)(4,1)S(1)} %fusion.33) | copy-start | bytes 442372
  23.8 14.7 %copy-start.14 = (bf16[128,1024]{0,1:T(8,128)(2,1)}, bf16[128,1024]{0,1:T(8,128)(2,1)S(1)}, u32[]{:S(2)}) copy-start(bf16[128,1024]{0,1:T(8,128)(2,1)S(1)} %get-tuple-element.120) | copy-start | bytes 786436
  31.7 3.9 %copy-start.9 = (bf16[1152,512]{0,1:T(8,128)(2,1)}, bf16[1152,512]{0,1:T(8,128)(2,1)S(1)}, u32[]{:S(2)}) copy-start(bf16[1152,512]{0,1:T(8,128)(2,1)S(1)} %get-tuple-element.116) | copy-start | bytes 3538948
  38.5 1.4 copy-start
  41.8 1.7 copy-start.7
  41.8 1.7 copy-start.17
  41.8 1.7 copy-start.23
  47.4 3.0 %copy-start.12 = (bf16[128,1024]{0,1:T(8,128)(2,1)S(1)}, bf16[128,1024]{0,1:T(8,128)(2,1)}, u32[]{:S(2)}) copy-start(bf16[128,1024]{0,1:T(8,128)(2,1)} %get-tuple-element.119) | copy-start | bytes 786436
  56.6 59.5 %collective-permute-start.9 = (bf16[1,128,1024]{2,1,0:T(8,128)(2,1)}, bf16[1,128,1024]{2,1,0:T(8,128)(2,1)}, u32[]{:S(2)}, u32[]{:S(2)}) collective-permute-start(bf16[1,128,1024]{2,1,0:T(8,128)(2,1)} %get-tuple-element.107), channel_id=1, source_target_pairs={{1,0},{2,1},{3,2},{5,4},{6,5},{7,6},{9,8},{10,9},{11,10},{13,12},{... | collective-permute-start | bytes 786440 | tf_op jit(solution)/shard_map/ppermute | solution.py:16
  57.9 58.2 %collective-permute-start.10 = (bf16[1,128,1024]{2,1,0:T(8,128)(2,1)}, bf16[1,128,1024]{2,1,0:T(8,128)(2,1)}, u32[]{:S(2)}, u32[]{:S(2)}) collective-permute-start(bf16[1,128,1024]{2,1,0:T(8,128)(2,1)} %get-tuple-element.108), channel_id=1, source_target_pairs={{2,0},{3,1},{6,4},{7,5},{10,8},{11,9},{14,12},{15,13},{18,16},{19,... | collective-permute-start | bytes 786440 | tf_op jit(solution)/shard_map/ppermute | solution.py:16
  59.2 57.0 %collective-permute-start.11 = (bf16[1,128,1024]{2,1,0:T(8,128)(2,1)}, bf16[1,128,1024]{2,1,0:T(8,128)(2,1)}, u32[]{:S(2)}, u32[]{:S(2)}) collective-permute-start(bf16[1,128,1024]{2,1,0:T(8,128)(2,1)} %get-tuple-element.109), channel_id=1, source_target_pairs={{3,0},{7,4},{11,8},{15,12},{19,16},{23,20},{27,24},{31,28}} | collective-permute-start | bytes 786440 | tf_op jit(solution)/shard_map/ppermute | solution.py:16
  103.0 70.6 %all-to-all-start = ((bf16[4,2,86016]{2,1,0:T(2,128)(2,1)}), bf16[4,2,86016]{2,1,0:T(2,128)(2,1)}, u32[]{:S(2)}, u32[]{:S(2)}) async-start(bf16[4,2,86016]{2,1,0:T(2,128)(2,1)} %reshape.143), calls=%async_computation | async-start | bytes 2752512 | tf_op jit(solution)/shard_map/all_to_all | solution.py:151
  116.2 67.3 %all-gather.3.cloned.1.call-start = ((), (), s32[]{:S(2)}) async-start(), calls=%async_computation.2 | async-start | bytes 1310720 | tf_op jit(solution)/shard_map/all_gather | solution.py:153
  118.2 161.0 %reduce-scatter.4.cloned.1.call-start = ((), (), s32[]{:S(2)}) async-start(), calls=%async_computation.3 | async-start | bytes 3244032
  119.4 42.4 %collective-permute-start.3 = (bf16[1,128,1024]{1,2,0:T(8,128)(2,1)S(1)}, bf16[1,128,1024]{1,2,0:T(8,128)(2,1)S(1)}, u32[]{:S(2)}, u32[]{:S(2)}) collective-permute-start(bf16[1,128,1024]{1,2,0:T(8,128)(2,1)S(1)} %copy.109), channel_id=1, source_target_pairs={{0,3},{4,7},{8,11},{12,15},{16,19},{20,23},{24,27},{28,31}} | collective-permute-start | bytes 786440 | tf_op jit(solution)/shard_map/ppermute | solution.py:16
  125.2 46.9 %collective-permute-start.5 = (bf16[1,128,1024]{1,2,0:T(8,128)(2,1)S(1)}, bf16[1,128,1024]{1,2,0:T(8,128)(2,1)S(1)}, u32[]{:S(2)}, u32[]{:S(2)}) collective-permute-start(bf16[1,128,1024]{1,2,0:T(8,128)(2,1)S(1)} %copy.109), channel_id=1, source_target_pairs={{0,1},{1,2},{2,3},{4,5},{5,6},{6,7},{8,9},{9,10},{10,11},{12,13},{... | collective-permute-start | bytes 786440 | tf_op jit(solution)/shard_map/ppermute | solution.py:16
  126.5 44.8 %collective-permute-start.4 = (bf16[1,128,1024]{1,2,0:T(8,128)(2,1)S(1)}, bf16[1,128,1024]{1,2,0:T(8,128)(2,1)S(1)}, u32[]{:S(2)}, u32[]{:S(2)}) collective-permute-start(bf16[1,128,1024]{1,2,0:T(8,128)(2,1)S(1)} %copy.109), channel_id=1, source_target_pairs={{0,2},{1,3},{4,6},{5,7},{8,10},{9,11},{12,14},{13,15},{16,18},{17,... | collective-permute-start | bytes 786440 | tf_op jit(solution)/shard_map/ppermute | solution.py:16
  215.1 3.1 %copy-start.15 = (bf16[128,1024]{0,1:T(8,128)(2,1)S(1)}, bf16[128,1024]{0,1:T(8,128)(2,1)}, u32[]{:S(2)}) copy-start(bf16[128,1024]{0,1:T(8,128)(2,1)} %copy-done.14) | copy-start | bytes 786436
  215.1 3.7 %slice-start = ((s8[4718592]{0:T(1024)(128)(4,1)}), s8[524288]{0:T(1024)(128)(4,1)S(1)}, s32[]{:S(2)}) async-start(s8[4718592]{0:T(1024)(128)(4,1)} %bitcast.200), calls=%async_computation.4 | async-start | bytes 1048576
  215.2 3.0 %copy-start.1 = (bf16[4,2,128,1152]{2,3,1,0:T(8,128)(2,1)S(1)}, bf16[4,2,128,1152]{2,3,1,0:T(8,128)(2,1)}, u32[]{:S(2)}) copy-start(bf16[4,2,128,1152]{2,3,1,0:T(8,128)(2,1)} %copy-done) | copy-start | bytes 7077892
  215.2 4.2 %slice-start.1 = ((s8[4718592]{0:T(1024)(128)(4,1)}), s8[4194304]{0:T(1024)(128)(4,1)S(1)}, s32[]{:S(2)}) async-start(s8[4718592]{0:T(1024)(128)(4,1)} %bitcast.200), calls=%async_computation.5 | async-start | bytes 8388608
  219.4 2.7 copy-start.20
  220.7 1.5 copy-start.2
  225.6 2.0 copy-start.11
  225.6 2.0 copy-start.13
  227.6 3.6 %copy-start.18 = (bf16[128,1024]{0,1:T(8,128)(2,1)S(1)}, bf16[128,1024]{0,1:T(8,128)(2,1)}, u32[]{:S(2)}) copy-start(bf16[128,1024]{0,1:T(8,128)(2,1)} %get-tuple-element.117) | copy-start | bytes 786436
  231.3 1.9 copy-start.4
  233.2 8.8 %copy-start.3 = (bf16[4,2,128,1152]{2,3,1,0:T(8,128)(2,1)S(1)}, bf16[4,2,128,1152]{2,3,1,0:T(8,128)(2,1)}, u32[]{:S(2)}) copy-start(bf16[4,2,128,1152]{2,3,1,0:T(8,128)(2,1)} %copy-done.2) | copy-start | bytes 7077892
  235.8 6.2 %copy-start.10 = (bf16[1152,512]{0,1:T(8,128)(2,1)S(1)}, bf16[1152,512]{0,1:T(8,128)(2,1)}, u32[]{:S(2)}) copy-start(bf16[1152,512]{0,1:T(8,128)(2,1)} %copy-done.9) | copy-start | bytes 3538948
  237.8 23.1 %collective-permute-start.6 = (bf16[1,128,1024]{2,1,0:T(8,128)(2,1)}, bf16[1,128,1024]{2,1,0:T(8,128)(2,1)}, u32[]{:S(2)}, u32[]{:S(2)}) collective-permute-start(bf16[1,128,1024]{2,1,0:T(8,128)(2,1)} %get-tuple-element.110), channel_id=1, source_target_pairs={{1,0},{2,1},{3,2},{5,4},{6,5},{7,6},{9,8},{10,9},{11,10},{13,12},{... | collective-permute-start | bytes 786440 | tf_op jit(solution)/shard_map/ppermute | solution.py:16
  239.1 38.2 %collective-permute-start.7 = (bf16[1,128,1024]{2,1,0:T(8,128)(2,1)}, bf16[1,128,1024]{2,1,0:T(8,128)(2,1)}, u32[]{:S(2)}, u32[]{:S(2)}) collective-permute-start(bf16[1,128,1024]{2,1,0:T(8,128)(2,1)} %get-tuple-element.111), channel_id=1, source_target_pairs={{2,0},{3,1},{6,4},{7,5},{10,8},{11,9},{14,12},{15,13},{18,16},{19,... | collective-permute-start | bytes 786440 | tf_op jit(solution)/shard_map/ppermute | solution.py:16
  240.4 2.9 %copy-start.5 = (bf16[4,2,128,1152]{2,3,1,0:T(8,128)(2,1)S(1)}, bf16[4,2,128,1152]{2,3,1,0:T(8,128)(2,1)}, u32[]{:S(2)}) copy-start(bf16[4,2,128,1152]{2,3,1,0:T(8,128)(2,1)} %copy-done.4) | copy-start | bytes 7077892
  240.4 2.9 %copy-start.8 = (bf16[1152,512]{0,1:T(8,128)(2,1)S(1)}, bf16[1152,512]{0,1:T(8,128)(2,1)}, u32[]{:S(2)}) copy-start(bf16[1152,512]{0,1:T(8,128)(2,1)} %get-tuple-element.115) | copy-start | bytes 3538948
  240.4 36.9 %collective-permute-start.8 = (bf16[1,128,1024]{2,1,0:T(8,128)(2,1)}, bf16[1,128,1024]{2,1,0:T(8,128)(2,1)}, u32[]{:S(2)}, u32[]{:S(2)}) collective-permute-start(bf16[1,128,1024]{2,1,0:T(8,128)(2,1)} %get-tuple-element.112), channel_id=1, source_target_pairs={{3,0},{7,4},{11,8},{15,12},{19,16},{23,20},{27,24},{31,28}} | collective-permute-start | bytes 786440 | tf_op jit(solution)/shard_map/ppermute | solution.py:16
  243.3 1.0 copy-start.16
  243.9 33.4 %copy-start.6 = (bf16[1152,512]{1,0:T(8,128)(2,1)S(1)}, bf16[1152,512]{1,0:T(8,128)(2,1)}, u32[]{:S(2)}) copy-start(bf16[1152,512]{1,0:T(8,128)(2,1)} %copy.128) | copy-start | bytes 3538948
Sparse Core Ops, SparseCore 0:
  119.1 44.2 all-gather.2
  215.3 59.8 reduce-scatter.3
where the time goes:
time: 289 us; the launch traced here: 288 us
  waiting for transfers between devices  77.7 us (27%)
  local copies, waits for them, and re-layouts  55.2 us (19%)
  other arithmetic  51.6 us (18%)
  matrix products  47.2 us (16%)
  starting transfers between devices  41.9 us (14%)
  between operations  14.5 us (5%)
    ppermute x12, waiting for transfers between devices, passed_along(): return lax.ppermute(shard, axis, pairs)  77.7 us
    unnamed x73, local copies, waits for them, and re-layouts  36.2 us
    unnamed x3, other arithmetic  31.3 us
    ppermute x12, starting transfers between devices, passed_along(): return lax.ppermute(shard, axis, pairs)  28.7 us
    dot_general x4, matrix products, one_shard(): jnp.einsum('td,tf->df', feature_rows, rows_here, preferred_element_type=j...  22.6 us
    all_to_all x1, starting transfers between devices, body(): lax.all_to_all(normed, 'ctx', split_axis=2, concat_axis=1, tiled=True)[0]  13.1 us
    sub x2, matrix products, band_core(): expanded = jnp.exp(attention_scores - highest)  7.7 us
    convert_element_type x2, other arithmetic, band_core(): reduced_precision_weight = weights_full.astype(jnp.bfloat16)  5.96 us
  transfers between devices with their start and end apart: 15, of which 5 were waited for; matrix products, arithmetic and copies ran while one was open for 31% of the time, Pallas kernels for 0%

commit v1 on v0

v1 whole, which is shorter than its diff:
```python
import functools

import jax
import jax.numpy as jnp
from jax import lax
from jax.experimental import pallas as pl
from jax.experimental.pallas import tpu as pltpu
from jax.sharding import PartitionSpec as P

HEAD_SIZE = 128
WINDOW = 1024
MESH = pl.DeviceIdType.MESH

query_scalar = 168.0


def flipped(index, mask):
    bit = 1
    while bit <= mask:
        if mask & bit:
            index = index + bit - 2 * bit * lax.rem(index // bit, 2)
        bit *= 2
    return index


def row_step(rows):
    return max(s for s in range(16, 449, 16) if rows % s == 0)


def mm(a, b, ca, cb):
    return lax.dot_general(a, b, (((ca,), (cb,)), ((), ())), preferred_element_type=jnp.float32)


def kernel(
    cfg,
    normed_ref, q_ref, k_ref, v_ref, do_ref, ids_ref,
    dq_ref, dk_ref, dv_ref, dw_ref,
    kbuf, vbuf, dk_out, dv_out, dk_in, dv_in, own_dk, own_dv, bias,
    nbuf, gbuf, w_own, w_send, w_sib, r_send, r_up, r_down,
    kv_send, kv_recv, back_send, back_recv, n_send, n_recv, g_send, g_recv, s_send, s_recv,
    u_send, u_recv, d_send, d_recv,
):
    chain, nd, count, blocks, chunks, heads, ratio, window = cfg
    c = lax.axis_index("ctx")
    d = lax.axis_index("dp")
    chips = nd // 2
    m, core = d // 2, lax.rem(d, 2)
    wide = heads * HEAD_SIZE
    scale = query_scalar ** (-0.5)
    features = normed_ref.shape[1]
    has_next, has_prev = c < chain - 1, c > 0

    def chip_at(mask):
        return {"dp": flipped(m, mask) * 2 + core}

    sibling = {"dp": m * 2 + 1 - core}
    after, before = {"ctx": c + 1}, {"ctx": c - 1}

    barrier = pltpu.get_barrier_semaphore()

    @pl.when(has_next)
    def _():
        pl.semaphore_signal(barrier, inc=1, device_id=after, device_id_type=MESH)

    @pl.when(has_prev)
    def _():
        pl.semaphore_signal(barrier, inc=1, device_id=before, device_id_type=MESH)

    for r in range(1, chips):
        pl.semaphore_signal(barrier, inc=1, device_id=chip_at(r), device_id_type=MESH)
    pl.semaphore_signal(barrier, inc=1, device_id=sibling, device_id_type=MESH)

    for s in range(1, blocks):
        @pl.when(c < s)
        def _():
            kbuf[s - 1] = jnp.zeros_like(kbuf[s - 1])
            vbuf[s - 1] = jnp.zeros_like(vbuf[s - 1])

    own_ids = ids_ref[:, pl.ds(pl.multiple_of(c * count, count), count)]
    query_ids = jnp.transpose(jnp.broadcast_to(own_ids, (count, count)))
    row = lax.broadcasted_iota(jnp.int32, (count, count), 0)
    col = lax.broadcasted_iota(jnp.int32, (count, count), 1)
    for s in range(blocks):
        at = jnp.maximum(c - s, 0)
        key_ids = ids_ref[:, pl.ds(pl.multiple_of(at * count, count), count)]
        offset = row - col + s * count
        good = (query_ids == key_ids) & (offset >= 0) & (offset < window) & (offset <= c * count + row)
        bias[:, s * count : (s + 1) * count] = jnp.where(good, 0.0, -jnp.inf)

    pl.semaphore_wait(barrier, has_next.astype(jnp.int32) + has_prev.astype(jnp.int32) + chips)

    def remote(src, dst, send, recv, where):
        return pltpu.make_async_remote_copy(
            src_ref=src, dst_ref=dst, send_sem=send, recv_sem=recv, device_id=where, device_id_type=MESH
        )

    def kv_copy(h, s, i):
        cols = pl.ds(pl.multiple_of(h * wide, wide), wide)
        own, buf = ((k_ref, kbuf), (v_ref, vbuf))[i]
        return remote(
            (own if s == 1 else buf.at[s - 2]).at[:, cols], buf.at[s - 1].at[:, cols],
            kv_send.at[h, s - 1, i], kv_recv.at[h, s - 1, i], after,
        )

    def kv_copies(h, s):
        return [kv_copy(h, s, i) for i in range(2)]

    def back_copy(h, s, i):
        cols = pl.ds(pl.multiple_of(h * wide, wide), wide)
        src, dst = ((dv_out, dv_in), (dk_out, dk_in))[i]
        return remote(
            src.at[s - 1].at[:, cols], dst.at[s - 1].at[:, cols],
            back_send.at[h, s - 1, i], back_recv.at[h, s - 1, i], before,
        )

    def send_own(h):
        @pl.when(has_next)
        def _():
            for copy in kv_copies(h, 1):
                copy.start()

    def forward(h):
        for s in range(1, blocks):
            @pl.when(c >= s)
            def _():
                for copy in kv_copies(h, s):
                    copy.wait_recv()

            if s + 1 < blocks:
                @pl.when((c >= s) & has_next)
                def _():
                    for copy in kv_copies(h, s + 1):
                        copy.start()

    half = (features // 256) * 128
    parts = ((0, half), (half, features - half))

    def n_copy(r, part, src, to):
        lo, size = parts[part]
        return remote(
            src.at[:, lo : lo + size], nbuf.at[r - 1].at[:, lo : lo + size],
            n_send.at[r - 1, part], n_recv.at[r - 1, part], chip_at(to),
        )

    relay = chips == 4

    def n_first():
        if relay:
            for r, part in ((1, 0), (2, 1), (1, 1), (2, 0)):
                n_copy(r, part, normed_ref, r).start()
        else:
            for r in range(1, chips):
                for part in range(2):
                    n_copy(r, part, normed_ref, r).start()

    def n_relay():
        if relay:
            n_copy(1, 0, normed_ref, 1).wait_recv()
            n_copy(3, 0, nbuf.at[0], 2).start()
            n_copy(2, 1, normed_ref, 2).wait_recv()
            n_copy(3, 1, nbuf.at[1], 1).start()

    def n_finish():
        for r in range(1, chips):
            for part in range(2):
                copy = n_copy(r, part, normed_ref, r)
                if not (relay and (r, part) in ((1, 0), (2, 1))):
                    copy.wait_recv()
                copy.wait_send()

    def compute(h):
        for g in range(heads):
            head = h * heads + g
            kv_cols = pl.ds(pl.multiple_of(head * HEAD_SIZE, HEAD_SIZE), HEAD_SIZE)

            def stacked(ref):
                return jnp.concatenate(
                    [
                        ref[:, pl.ds(pl.multiple_of((head * ratio + z) * HEAD_SIZE, HEAD_SIZE), HEAD_SIZE)]
                        for z in range(ratio)
                    ],
                    axis=0,
                )

            q, do = stacked(q_ref), stacked(do_ref)
            keys = jnp.concatenate([k_ref[:, kv_cols]] + [kbuf[s - 1, :, kv_cols] for s in range(1, blocks)], axis=0)
            values = jnp.concatenate([v_ref[:, kv_cols]] + [vbuf[s - 1, :, kv_cols] for s in range(1, blocks)], axis=0)
            scores = mm(q, keys, 1, 1) * scale
            scores = scores + jnp.concatenate([bias[...]] * ratio, axis=0)
            top = jnp.max(scores, axis=1, keepdims=True)
            expanded = jnp.exp(scores - top)
            weights = expanded * (1.0 / jnp.sum(expanded, axis=1, keepdims=True))
            low = weights.astype(jnp.bfloat16)
            grad_probs = mm(do, values, 1, 1)
            delta = jnp.sum(low.astype(jnp.float32) * grad_probs, axis=1, keepdims=True)
            grad_scores = (weights * (grad_probs - delta)).astype(jnp.bfloat16)
            dq = (mm(grad_scores, keys, 1, 0) * scale).astype(jnp.bfloat16)
            for z in range(ratio):
                dq_ref[:, pl.ds(pl.multiple_of((head * ratio + z) * HEAD_SIZE, HEAD_SIZE), HEAD_SIZE)] = dq[
                    z * count : (z + 1) * count
                ]
            dv = mm(low, do, 0, 0)
            dk = mm(grad_scores, q, 0, 0) * scale
            for s in range(blocks):
                own_dv[s, :, kv_cols] = dv[s * count : (s + 1) * count]
                own_dk[s, :, kv_cols] = dk[s * count : (s + 1) * count]

    def give_back(h, last, which):
        cols = pl.ds(pl.multiple_of(h * wide, wide), wide)
        own, into, out, final = ((own_dv, dv_in, dv_out, dv_ref), (own_dk, dk_in, dk_out, dk_ref))[which]
        for s in range(blocks - 1, -1, -1):
            takes = not last and s + 1 < blocks

            def total():
                value = own[s, :, cols]
                if takes:
                    value = value + into[s, :, cols].astype(jnp.float32)
                return value.astype(jnp.bfloat16)

            if s > 0:
                @pl.when(c >= s)
                def _():
                    if takes:
                        back_copy(h, s + 1, which).wait_recv()
                    out[s - 1, :, cols] = total()
                    back_copy(h, s, which).start()
            else:
                if takes:
                    back_copy(h, 1, which).wait_recv()
                final[:, cols] = total()

    send_own(0)
    if chunks > 1:
        send_own(1)
    n_first()
    forward(0)

    def chunk(h, carry):
        compute(h)

        @pl.when((c == chain - 1) & (h < chunks - 1))
        def _():
            give_back(h, True, 0)
            give_back(h, True, 1)

        @pl.when(h + 2 < chunks)
        def _():
            send_own(h + 2)

        @pl.when(h + 1 < chunks)
        def _():
            forward(h + 1)

        @pl.when(has_next & (h < chunks - 1))
        def _():
            give_back(h, False, 0)
            give_back(h, False, 1)

        @pl.when(h == min(1, chunks - 1))
        def _():
            n_relay()

        return carry

    lax.fori_loop(0, chunks, chunk, 0)

    end = chunks - 1

    @pl.when(c == chain - 1)
    def _():
        give_back(end, True, 0)
        give_back(end, True, 1)

    @pl.when(has_next)
    def _():
        give_back(end, False, 0)

    pair = gbuf.shape[2]
    cw = pair // 2

    def g_copy(r):
        to = flipped(m, r)
        return remote(
            dv_ref.at[:, pl.ds(pl.multiple_of(to * pair, pair), pair)], gbuf.at[r - 1],
            g_send.at[r - 1], g_recv.at[r - 1], chip_at(r),
        )

    for r in range(1, chips):
        g_copy(r).start()

    @pl.when(has_next)
    def _():
        give_back(end, False, 1)

    n_finish()
    for r in range(1, chips):
        g_copy(r).wait_recv()

    own_g = dv_ref[:, pl.ds(pl.multiple_of(m * pair, pair), pair)]
    tile = 384 if features % 384 == 0 else 128

    def w_tile(t, carry):
        cols = pl.ds(pl.multiple_of(t * tile, tile), tile)
        acc = mm(normed_ref[:, cols], own_g, 0, 0)
        for r in range(1, chips):
            acc = acc + mm(nbuf[r - 1, :, cols], gbuf[r - 1], 0, 0)
        low = acc[:, :cw]
        high = acc[:, cw:] if cw % 128 == 0 else pltpu.roll(acc, cw, 1)[:, :cw]
        first = core == 0
        w_own[cols, :] = jnp.where(first, low, high)
        w_send[cols, :] = jnp.where(first, high, low).astype(jnp.bfloat16)
        return carry

    lax.fori_loop(0, features // tile, w_tile, 0)

    rows = features // chain

    def s_copy(r):
        span = pl.ds(r * rows, rows)
        return remote(w_send.at[span], w_sib.at[span], s_send.at[r], s_recv.at[r], sibling)

    order = []
    for t in range(chain):
        order += [chain - 1 - t, t]
    order = list(dict.fromkeys(order))
    for r in order:
        s_copy(r).start()

    step = row_step(rows)

    def u_copy(r):
        return remote(r_send.at[r], r_up.at[r], u_send.at[r], u_recv.at[r], after)

    def d_copy(r):
        return remote(r_send.at[r], r_down.at[r], d_send.at[r], d_recv.at[r], before)

    def sums(r, extra, put):
        def one(t, carry):
            lo = pl.multiple_of(t * step, step)
            base = pl.ds(pl.multiple_of(r * rows + t * step, 16), step)
            value = w_own[base, :] + w_sib[base, :].astype(jnp.float32)
            for ref in extra:
                value = value + ref[r, pl.ds(lo, step), :].astype(jnp.float32)
            put(pl.ds(lo, step), value)
            return carry

        lax.fori_loop(0, rows // step, one, 0)

    def put_send(r):
        def put(span, value):
            r_send[r, span, :] = value.astype(jnp.bfloat16)
        return put

    arrived = set()

    def sib_ready(r):
        if r not in arrived:
            arrived.add(r)
            s_copy(r).wait_recv()

    def up_piece(r):
        @pl.when(c == 0)
        def _():
            sums(r, (), put_send(r))
            u_copy(r).start()

        @pl.when((c > 0) & (c < r))
        def _():
            u_copy(r).wait_recv()
            sums(r, (r_up,), put_send(r))
            u_copy(r).start()

    def down_piece(r):
        @pl.when(c == chain - 1)
        def _():
            sums(r, (), put_send(r))
            d_copy(r).start()

        @pl.when((c < chain - 1) & (c > r))
        def _():
            d_copy(r).wait_recv()
            sums(r, (r_down,), put_send(r))
            d_copy(r).start()

    for t in range(chain - 1):
        sib_ready(chain - 1 - t)
        up_piece(chain - 1 - t)
        sib_ready(t)
        down_piece(t)
    for r in range(chain):
        sib_ready(r)

    final_scale = (count * chain * nd) ** (-0.5)

    def put_final(span, value):
        dw_ref[span, :] = (value * final_scale).astype(jnp.bfloat16)

    @pl.when(has_prev)
    def _():
        u_copy(c).wait_recv()

    @pl.when(has_next)
    def _():
        d_copy(c).wait_recv()

    @pl.when(c == 0)
    def _():
        sums(c, (r_down,), put_final)

    @pl.when(c == chain - 1)
    def _():
        sums(c, (r_up,), put_final)

    @pl.when(has_prev & has_next)
    def _():
        sums(c, (r_up, r_down), put_final)

    def drain(h, carry):
        for s in range(1, blocks):
            @pl.when(has_next & (c >= s - 1))
            def _():
                for copy in kv_copies(h, s):
                    copy.wait_send()

            @pl.when(c >= s)
            def _():
                for i in range(2):
                    back_copy(h, s, i).wait_send()
        return carry

    lax.fori_loop(0, chunks, drain, 0)
    for r in range(1, chips):
        g_copy(r).wait_send()
    for r in range(chain):
        s_copy(r).wait_send()

        @pl.when(c < r)
        def _():
            u_copy(r).wait_send()

        @pl.when(c > r)
        def _():
            d_copy(r).wait_send()


def body(normed, queries, keys, values, out_grad, segment_ids):
    count = queries.shape[1]
    width = keys.shape[2]
    features = normed.shape[2]
    chain, nd = lax.axis_size("ctx"), lax.axis_size("dp")
    chips = nd // 2
    blocks = min(-(-WINDOW // count), chain - 1) + 1
    groups = width // HEAD_SIZE
    heads = max(1, groups // 4)
    chunks = groups // heads
    ratio = queries.shape[2] // width
    cw = width // nd
    rows = features // chain
    bf, f32 = jnp.bfloat16, jnp.float32
    vm = pltpu.VMEM
    dma = pltpu.SemaphoreType.DMA
    back = blocks - 1
    cfg = (chain, nd, count, blocks, chunks, heads, ratio, WINDOW)
    out = pl.pallas_call(
        functools.partial(kernel, cfg),
        out_shape=(
            jax.ShapeDtypeStruct(queries.shape[1:], bf),
            jax.ShapeDtypeStruct(keys.shape[1:], bf),
            jax.ShapeDtypeStruct(keys.shape[1:], bf),
            jax.ShapeDtypeStruct((rows, cw), bf),
        ),
        in_specs=[pl.BlockSpec(memory_space=vm)] * 6,
        out_specs=(pl.BlockSpec(memory_space=vm),) * 4,
        scratch_shapes=[
            vm((back, count, width), bf), vm((back, count, width), bf),
            vm((back, count, width), bf), vm((back, count, width), bf),
            vm((back, count, width), bf), vm((back, count, width), bf),
            vm((blocks, count, width), f32), vm((blocks, count, width), f32),
            vm((count, blocks * count), f32),
            vm((chips - 1, count, features), bf), vm((chips - 1, count, 2 * cw), bf),
            vm((features, cw), f32), vm((features, cw), bf), vm((features, cw), bf),
            vm((chain, rows, cw), bf), vm((chain, rows, cw), bf), vm((chain, rows, cw), bf),
            dma((chunks, back, 2)), dma((chunks, back, 2)), dma((chunks, back, 2)), dma((chunks, back, 2)),
            dma((chips - 1, 2)), dma((chips - 1, 2)), dma((chips - 1,)), dma((chips - 1,)),
            dma((chain,)), dma((chain,)), dma((chain,)), dma((chain,)), dma((chain,)), dma((chain,)),
        ],
        compiler_params=pltpu.CompilerParams(
            collective_id=0, has_side_effects=True, vmem_limit_bytes=64000 * 1024
        ),
    )(normed[0], queries[0], keys[0], values[0], out_grad[0], segment_ids)
    return out[0][None], out[1][None], out[2][None], out[3]


def solution(mesh):
    placed = (P("dp", "ctx", None),) * 5 + (P("dp", None),)
    return jax.shard_map(
        body,
        mesh=mesh,
        in_specs=placed,
        out_specs=(
            P("dp", "ctx", None),
            P("dp", "ctx", None),
            P("dp", "ctx", None),
            P("ctx", "dp"),
        ),
        check_vma=False,
    )
```

time: 289 us -> 125 us (0.43)
  Pallas kernels: 0 us -> 119 us
  waiting for transfers between devices: 77.7 us -> 0 us
  other arithmetic: 51.6 us -> 0 us
  local copies, waits for them, and re-layouts: 55.2 us -> 5.05 us
  matrix products: 47.2 us -> 0 us
  starting transfers between devices: 41.9 us -> 0 us
  between operations: 14.5 us -> 0.66 us
    pallas_call x0 -> x1, Pallas kernels: none -> 119 us  [body(): pl.pallas_call(functools.partial(kernel, cfg), out_shape=(jax.ShapeDtypeS...]
    ppermute x12 -> x0, waiting for transfers between devices: 77.7 us -> none  [passed_along(): return lax.ppermute(shard, axis, pairs)]
    dot_general x14 -> x0, matrix products: 39.5 us -> none  [the longest x4 22.6 us: one_shard(): jnp.einsum('td,tf->df', feature_rows, rows_here, preferred_element_type=j...]
    unnamed x3 -> x0, other arithmetic: 31.3 us -> none
    unnamed x73 -> x8, local copies, waits for them, and re-layouts: 36.2 us -> 5.05 us
    ppermute x12 -> x0, starting transfers between devices: 28.7 us -> none  [passed_along(): return lax.ppermute(shard, axis, pairs)]
    convert_element_type x5 -> x0, other arithmetic: 13.3 us -> none  [the longest x2 5.96 us: band_core(): reduced_precision_weight = weights_full.astype(jnp.bfloat16)]
    all_to_all x1 -> x0, starting transfers between devices: 13.1 us -> none  [body(): lax.all_to_all(normed, 'ctx', split_axis=2, concat_axis=1, tiled=True)[0]]
  transfers between devices with their start and end apart: 15 -> 0, of which waited for: 5 -> 0; matrix products, arithmetic and copies ran while one was open for 31% -> 0% of each run, Pallas kernels for 0% -> 0%
where the time goes in v1:
time: 125 us; the launch traced here: 124 us
  Pallas kernels  119 us (95%)
  local copies, waits for them, and re-layouts  5.05 us (4%)
    pallas_call x1, Pallas kernels, body(): pl.pallas_call(functools.partial(kernel, cfg), out_shape=(jax.ShapeDtypeS...  119 us
    unnamed x8, local copies, waits for them, and re-layouts  5.05 us

profile of v1, /device:TPU:0, one launch (start us, length us, event | category | flops | bytes accessed | tf_op | source)
XLA Modules:
  0.0 124.5 jit_solution(9934934557289131772)
XLA Ops:
  0.6 118.8 %shard_map.93 = (bf16[128,2048]{1,0:T(8,128)(2,1)}, bf16[128,1024]{1,0:T(8,128)(2,1)}, bf16[128,1024]{1,0:T(8,128)(2,1)}, bf16[1344,128]{1,0:T(8,128)(2,1)}) custom-call(bf16[128,5376]{1,0:T(8,128)(2,1)} %bitcast.8, bf16[128,2048]{1,0:T(8,128)(2,1)} %bitcast.9, bf16[128,1024]{1,0:T(8,128)(2,1)} %bitcast.12, bf16[128,1024]{1,0:T(8,128)(2,1)} %bitcast.13, ...), custom_call_target="tpu_custom_call" | custom-call | tf_op jit(solution)/shard_map/pallas_call | solution.py:464
  119.4 0.0 copy-start.1
  119.4 0.0 copy-start
  119.4 1.9 %copy.14 = bf16[1,128,2048]{2,1,0:T(8,128)(2,1)} copy(bf16[1,128,2048]{2,1,0:T(8,128)(2,1)} %bitcast.11) | data formatting | bytes 1048576
  121.4 1.7 %copy.15 = bf16[1,128,1024]{2,1,0:T(8,128)(2,1)} copy(bf16[1,128,1024]{2,1,0:T(8,128)(2,1)} %bitcast.15) | data formatting | bytes 524288
  123.0 0.0 copy-done.1
  123.0 0.7 copy.16
  123.8 0.0 copy-done
  123.8 0.7 copy.17
Async XLA Ops:
  119.4 3.6 %copy-start.1 = (bf16[128,1024]{1,0:T(8,128)(2,1)S(1)}, bf16[128,1024]{1,0:T(8,128)(2,1)}, u32[]{:S(2)}) copy-start(bf16[128,1024]{1,0:T(8,128)(2,1)} %get-tuple-element.10) | copy-start | bytes 786436
  119.4 4.3 %copy-start = (bf16[1344,128]{1,0:T(8,128)(2,1)S(1)}, bf16[1344,128]{1,0:T(8,128)(2,1)}, u32[]{:S(2)}) copy-start(bf16[1344,128]{1,0:T(8,128)(2,1)} %get-tuple-element.19) | copy-start | bytes 1032196

commit v2 on v1

--- a/solution.py
+++ b/solution.py
@@ -21,10 +21,6 @@
             index = index + bit - 2 * bit * lax.rem(index // bit, 2)
         bit *= 2
     return index
-
-
-def row_step(rows):
-    return max(s for s in range(16, 449, 16) if rows % s == 0)
 
 
 def mm(a, b, ca, cb):
@@ -229,42 +225,44 @@
                     back_copy(h, 1, which).wait_recv()
                 final[:, cols] = total()
 
+    lag = jnp.where(c == chain - 1, 0, jnp.where(c == chain - 2, min(2, chunks), chunks))
+    end = chunks - 1
     send_own(0)
     if chunks > 1:
         send_own(1)
     n_first()
-    forward(0)
-
-    def chunk(h, carry):
-        compute(h)
-
-        @pl.when((c == chain - 1) & (h < chunks - 1))
-        def _():
-            give_back(h, True, 0)
-            give_back(h, True, 1)
-
-        @pl.when(h + 2 < chunks)
-        def _():
-            send_own(h + 2)
-
-        @pl.when(h + 1 < chunks)
-        def _():
-            forward(h + 1)
-
-        @pl.when(has_next & (h < chunks - 1))
-        def _():
-            give_back(h, False, 0)
-            give_back(h, False, 1)
-
-        @pl.when(h == min(1, chunks - 1))
+
+    def chunk(i, carry):
+        @pl.when(i < chunks)
+        def _():
+            forward(i)
+
+            @pl.when(i + 2 < chunks)
+            def _():
+                send_own(i + 2)
+
+            compute(i)
+
+        j = i - lag
+        turn = (j >= 0) & (j < end)
+
+        @pl.when(turn & (c == chain - 1))
+        def _():
+            give_back(j, True, 0)
+            give_back(j, True, 1)
+
+        @pl.when(turn & has_next)
+        def _():
+            give_back(j, False, 0)
+            give_back(j, False, 1)
+
+        @pl.when(i == min(2, end))
         def _():
             n_relay()
 
         return carry
 
-    lax.fori_loop(0, chunks, chunk, 0)
-
-    end = chunks - 1
+    lax.fori_loop(0, 2 * chunks, chunk, 0)
 
     @pl.when(c == chain - 1)
     def _():
@@ -314,106 +312,106 @@
     lax.fori_loop(0, features // tile, w_tile, 0)
 
     rows = features // chain
-
-    def s_copy(r):
-        span = pl.ds(r * rows, rows)
-        return remote(w_send.at[span], w_sib.at[span], s_send.at[r], s_recv.at[r], sibling)
-
-    order = []
-    for t in range(chain):
-        order += [chain - 1 - t, t]
-    order = list(dict.fromkeys(order))
-    for r in order:
-        s_copy(r).start()
-
-    step = row_step(rows)
-
-    def u_copy(r):
-        return remote(r_send.at[r], r_up.at[r], u_send.at[r], u_recv.at[r], after)
-
-    def d_copy(r):
-        return remote(r_send.at[r], r_down.at[r], d_send.at[r], d_recv.at[r], before)
-
-    def sums(r, extra, put):
-        def one(t, carry):
-            lo = pl.multiple_of(t * step, step)
-            base = pl.ds(pl.multiple_of(r * rows + t * step, 16), step)
-            value = w_own[base, :] + w_sib[base, :].astype(jnp.float32)
-            for ref in extra:
-                value = value + ref[r, pl.ds(lo, step), :].astype(jnp.float32)
-            put(pl.ds(lo, step), value)
-            return carry
-
-        lax.fori_loop(0, rows // step, one, 0)
-
-    def put_send(r):
-        def put(span, value):
-            r_send[r, span, :] = value.astype(jnp.bfloat16)
-        return put
-
-    arrived = set()
-
-    def sib_ready(r):
-        if r not in arrived:
-            arrived.add(r)
-            s_copy(r).wait_recv()
-
-    def up_piece(r):
+    subs = r_send.shape[0] // chain
+    step = rows // subs
+    whole = chain * subs
+
+    def s_copy(p):
+        span = pl.ds(pl.multiple_of(p * step, 16), step)
+        return remote(w_send.at[span], w_sib.at[span], s_send.at[p], s_recv.at[p], sibling)
+
+    def u_copy(p):
+        return remote(r_send.at[p], r_up.at[p], u_send.at[p], u_recv.at[p], after)
+
+    def d_copy(p):
+        return remote(r_send.at[p], r_down.at[p], d_send.at[p], d_recv.at[p], before)
+
+    def up_index(u):
+        return (chain - 1 - u // subs) * subs + lax.rem(u, subs)
+
+    def send_sib(t, carry):
+        flip = jnp.where(c < chain - c, up_index(t), t)
+        s_copy(flip).start()
+        return carry
+
+    lax.fori_loop(0, whole, send_sib, 0)
+
+    def sums(p, extra):
+        base = pl.ds(pl.multiple_of(p * step, 16), step)
+        value = w_own[base, :] + w_sib[base, :].astype(jnp.float32)
+        for ref in extra:
+            value = value + ref[p].astype(jnp.float32)
+        return value
+
+    def reduce_step(tau, carry):
+        u = tau - 2 * c
+        v = tau - 2 * (chain - 1 - c)
+
+        @pl.when((u >= 0) & (u < (chain - 1 - c) * subs))
+        def _():
+            p = up_index(u)
+            s_copy(p).wait_recv()
+
+            @pl.when(c == 0)
+            def _():
+                r_send[p] = sums(p, ()).astype(jnp.bfloat16)
+
+            @pl.when(c > 0)
+            def _():
+                u_copy(p).wait_recv()
+                r_send[p] = sums(p, (r_up,)).astype(jnp.bfloat16)
+
+            u_copy(p).start()
+
+        @pl.when((v >= 0) & (v < c * subs))
+        def _():
+            s_copy(v).wait_recv()
+
+            @pl.when(c == chain - 1)
+            def _():
+                r_send[v] = sums(v, ()).astype(jnp.bfloat16)
+
+            @pl.when(c < chain - 1)
+            def _():
+                d_copy(v).wait_recv()
+                r_send[v] = sums(v, (r_down,)).astype(jnp.bfloat16)
+
+            d_copy(v).start()
+
+        return carry
+
+    lax.fori_loop(0, (chain - 1) * (subs + 2), reduce_step, 0)
+
+    final_scale = (count * chain * nd) ** (-0.5)
+
+    def finish(t, carry):
+        p = c * subs + t
+        s_copy(p).wait_recv()
+        span = pl.ds(pl.multiple_of(t * step, 16), step)
+
+        @pl.when(has_prev)
+        def _():
+            u_copy(p).wait_recv()
+
+        @pl.when(has_next)
+        def _():
+            d_copy(p).wait_recv()
+
         @pl.when(c == 0)
         def _():
-            sums(r, (), put_send(r))
-            u_copy(r).start()
-
-        @pl.when((c > 0) & (c < r))
-        def _():
-            u_copy(r).wait_recv()
-            sums(r, (r_up,), put_send(r))
-            u_copy(r).start()
-
-    def down_piece(r):
+            dw_ref[span, :] = (sums(p, (r_down,)) * final_scale).astype(jnp.bfloat16)
+
         @pl.when(c == chain - 1)
         def _():
-            sums(r, (), put_send(r))
-            d_copy(r).start()
-
-        @pl.when((c < chain - 1) & (c > r))
-        def _():
-            d_copy(r).wait_recv()
-            sums(r, (r_down,), put_send(r))
-            d_copy(r).start()
-
-    for t in range(chain - 1):
-        sib_ready(chain - 1 - t)
-        up_piece(chain - 1 - t)
-        sib_ready(t)
-        down_piece(t)
-    for r in range(chain):
-        sib_ready(r)
-
-    final_scale = (count * chain * nd) ** (-0.5)
-
-    def put_final(span, value):
-        dw_ref[span, :] = (value * final_scale).astype(jnp.bfloat16)
-
-    @pl.when(has_prev)
-    def _():
-        u_copy(c).wait_recv()
-
-    @pl.when(has_next)
-    def _():
-        d_copy(c).wait_recv()
-
-    @pl.when(c == 0)
-    def _():
-        sums(c, (r_down,), put_final)
-
-    @pl.when(c == chain - 1)
-    def _():
-        sums(c, (r_up,), put_final)
-
-    @pl.when(has_prev & has_next)
-    def _():
-        sums(c, (r_up, r_down), put_final)
+            dw_ref[span, :] = (sums(p, (r_up,)) * final_scale).astype(jnp.bfloat16)
+
+        @pl.when(has_prev & has_next)
+        def _():
+            dw_ref[span, :] = (sums(p, (r_up, r_down)) * final_scale).astype(jnp.bfloat16)
+
+        return carry
+
+    lax.fori_loop(0, subs, finish, 0)
 
     def drain(h, carry):
         for s in range(1, blocks):
@@ -431,16 +429,21 @@
     lax.fori_loop(0, chunks, drain, 0)
     for r in range(1, chips):
         g_copy(r).wait_send()
-    for r in range(chain):
-        s_copy(r).wait_send()
-
-        @pl.when(c < r)
-        def _():
-            u_copy(r).wait_send()
-
-        @pl.when(c > r)
-        def _():
-            d_copy(r).wait_send()
+
+    def drain_pieces(p, carry):
+        s_copy(p).wait_send()
+
+        @pl.when(p >= (c + 1) * subs)
+        def _():
+            u_copy(p).wait_send()
+
+        @pl.when(p < c * subs)
+        def _():
+            d_copy(p).wait_send()
+
+        return carry
+
+    lax.fori_loop(0, whole, drain_pieces, 0)
 
 
 def body(normed, queries, keys, values, out_grad, segment_ids):
@@ -456,6 +459,8 @@
     ratio = queries.shape[2] // width
     cw = width // nd
     rows = features // chain
+    subs = max(n for n in range(1, 5) if rows % (16 * n) == 0)
+    pieces = chain * subs
     bf, f32 = jnp.bfloat16, jnp.float32
     vm = pltpu.VMEM
     dma = pltpu.SemaphoreType.DMA
@@ -479,10 +484,10 @@
             vm((count, blocks * count), f32),
             vm((chips - 1, count, features), bf), vm((chips - 1, count, 2 * cw), bf),
             vm((features, cw), f32), vm((features, cw), bf), vm((features, cw), bf),
-            vm((chain, rows, cw), bf), vm((chain, rows, cw), bf), vm((chain, rows, cw), bf),
+            vm((pieces, rows // subs, cw), bf), vm((pieces, rows // subs, cw), bf), vm((pieces, rows // subs, cw), bf),
             dma((chunks, back, 2)), dma((chunks, back, 2)), dma((chunks, back, 2)), dma((chunks, back, 2)),
             dma((chips - 1, 2)), dma((chips - 1, 2)), dma((chips - 1,)), dma((chips - 1,)),
-            dma((chain,)), dma((chain,)), dma((chain,)), dma((chain,)), dma((chain,)), dma((chain,)),
+            dma((pieces,)), dma((pieces,)), dma((pieces,)), dma((pieces,)), dma((pieces,)), dma((pieces,)),
         ],
         compiler_params=pltpu.CompilerParams(
             collective_id=0, has_side_effects=True, vmem_limit_bytes=64000 * 1024

time: 125 us -> 102 us (0.82)
  Pallas kernels: 119 us -> 95.7 us
    pallas_call x1, Pallas kernels: 119 us -> 95.7 us  [body(): pl.pallas_call(functools.partial(kernel, cfg), out_shape=(jax.ShapeDtypeS...]
where the time goes in v2:
time: 102 us; the launch traced here: 101 us
  Pallas kernels  95.7 us (94%)
  local copies, waits for them, and re-layouts  5.05 us (5%)
    pallas_call x1, Pallas kernels, body(): pl.pallas_call(functools.partial(kernel, cfg), out_shape=(jax.ShapeDtypeS...  95.7 us
    unnamed x8, local copies, waits for them, and re-layouts  5.05 us

profile of v2, /device:TPU:0, one launch (start us, length us, event | category | flops | bytes accessed | tf_op | source)
XLA Modules:
  0.0 101.4 jit_solution(11169062138767380742)
XLA Ops:
  0.6 95.7 %shard_map.93 = (bf16[128,2048]{1,0:T(8,128)(2,1)}, bf16[128,1024]{1,0:T(8,128)(2,1)}, bf16[128,1024]{1,0:T(8,128)(2,1)}, bf16[1344,128]{1,0:T(8,128)(2,1)}) custom-call(bf16[128,5376]{1,0:T(8,128)(2,1)} %bitcast.8, bf16[128,2048]{1,0:T(8,128)(2,1)} %bitcast.9, bf16[128,1024]{1,0:T(8,128)(2,1)} %bitcast.12, bf16[128,1024]{1,0:T(8,128)(2,1)} %bitcast.13, ...), custom_call_target="tpu_custom_call" | custom-call | tf_op jit(solution)/shard_map/pallas_call | solution.py:469
  96.4 0.0 copy-start.1
  96.4 0.0 copy-start
  96.4 1.9 %copy.14 = bf16[1,128,2048]{2,1,0:T(8,128)(2,1)} copy(bf16[1,128,2048]{2,1,0:T(8,128)(2,1)} %bitcast.11) | data formatting | bytes 1048576
  98.3 1.7 %copy.15 = bf16[1,128,1024]{2,1,0:T(8,128)(2,1)} copy(bf16[1,128,1024]{2,1,0:T(8,128)(2,1)} %bitcast.15) | data formatting | bytes 524288
  100.0 0.0 copy-done.1
  100.0 0.7 copy.16
  100.7 0.0 copy-done
  100.7 0.7 copy.17
Async XLA Ops:
  96.4 3.6 %copy-start.1 = (bf16[128,1024]{1,0:T(8,128)(2,1)S(1)}, bf16[128,1024]{1,0:T(8,128)(2,1)}, u32[]{:S(2)}) copy-start(bf16[128,1024]{1,0:T(8,128)(2,1)} %get-tuple-element.10) | copy-start | bytes 786436
  96.4 4.3 %copy-start = (bf16[1344,128]{1,0:T(8,128)(2,1)S(1)}, bf16[1344,128]{1,0:T(8,128)(2,1)}, u32[]{:S(2)}) copy-start(bf16[1344,128]{1,0:T(8,128)(2,1)} %get-tuple-element.19) | copy-start | bytes 1032196

commit v3 on v2

--- a/solution.py
+++ b/solution.py
@@ -32,7 +32,7 @@
     normed_ref, q_ref, k_ref, v_ref, do_ref, ids_ref,
     dq_ref, dk_ref, dv_ref, dw_ref,
     kbuf, vbuf, dk_out, dv_out, dk_in, dv_in, own_dk, own_dv, bias,
-    nbuf, gbuf, w_own, w_send, w_sib, r_send, r_up, r_down,
+    nbuf, gbuf, turned, w_own, w_send, w_sib, r_send, r_up, r_down,
     kv_send, kv_recv, back_send, back_recv, n_send, n_recv, g_send, g_recv, s_send, s_recv,
     u_send, u_recv, d_send, d_recv,
 ):
@@ -140,6 +140,17 @@
 
     relay = chips == 4
 
+    def turn_part(r, part):
+        src = normed_ref if r == 0 else nbuf.at[r - 1]
+        lo, size = parts[part]
+
+        def one(t, carry):
+            cols = pl.ds(pl.multiple_of(lo + t * 128, 128), 128)
+            turned[cols, r * count : (r + 1) * count] = jnp.transpose(src[:, cols])
+            return carry
+
+        lax.fori_loop(0, size // 128, one, 0, unroll=3)
+
     def n_first():
         if relay:
             for r, part in ((1, 0), (2, 1), (1, 1), (2, 0)):
@@ -155,6 +166,8 @@
             n_copy(3, 0, nbuf.at[0], 2).start()
             n_copy(2, 1, normed_ref, 2).wait_recv()
             n_copy(3, 1, nbuf.at[1], 1).start()
+            turn_part(1, 0)
+            turn_part(2, 1)
 
     def n_finish():
         for r in range(1, chips):
@@ -163,6 +176,9 @@
                 if not (relay and (r, part) in ((1, 0), (2, 1))):
                     copy.wait_recv()
                 copy.wait_send()
+        if relay:
+            for r, part in ((1, 1), (2, 0), (3, 0), (3, 1)):
+                turn_part(r, part)
 
     def compute(h):
         for g in range(heads):
@@ -225,12 +241,17 @@
                     back_copy(h, 1, which).wait_recv()
                 final[:, cols] = total()
 
-    lag = jnp.where(c == chain - 1, 0, jnp.where(c == chain - 2, min(2, chunks), chunks))
+    lag = jnp.where(c == chain - 1, 0, jnp.where(c == chain - 2, min(3, chunks), chunks))
     end = chunks - 1
+    relay_at = jnp.where(c == chain - 1, chunks // 2, end)
+    held = min(2, chunks)
     send_own(0)
     if chunks > 1:
         send_own(1)
     n_first()
+    if relay:
+        turn_part(0, 0)
+        turn_part(0, 1)
 
     def chunk(i, carry):
         @pl.when(i < chunks)
@@ -249,14 +270,20 @@
         @pl.when(turn & (c == chain - 1))
         def _():
             give_back(j, True, 0)
-            give_back(j, True, 1)
+
+            @pl.when(j < chunks - held)
+            def _():
+                give_back(j, True, 1)
 
         @pl.when(turn & has_next)
         def _():
             give_back(j, False, 0)
-            give_back(j, False, 1)
-
-        @pl.when(i == min(2, end))
+
+            @pl.when(j < chunks - held)
+            def _():
+                give_back(j, False, 1)
+
+        @pl.when(i == relay_at)
         def _():
             n_relay()
 
@@ -267,7 +294,6 @@
     @pl.when(c == chain - 1)
     def _():
         give_back(end, True, 0)
-        give_back(end, True, 1)
 
     @pl.when(has_next)
     def _():
@@ -286,9 +312,14 @@
     for r in range(1, chips):
         g_copy(r).start()
 
-    @pl.when(has_next)
-    def _():
-        give_back(end, False, 1)
+    for e in range(chunks - held, chunks):
+        @pl.when(c == chain - 1)
+        def _():
+            give_back(e, True, 1)
+
+        @pl.when(has_next)
+        def _():
+            give_back(e, False, 1)
 
     n_finish()
     for r in range(1, chips):
@@ -302,14 +333,19 @@
         acc = mm(normed_ref[:, cols], own_g, 0, 0)
         for r in range(1, chips):
             acc = acc + mm(nbuf[r - 1, :, cols], gbuf[r - 1], 0, 0)
+        w_store(cols, acc)
+        return carry
+
+    def w_store(cols, acc):
         low = acc[:, :cw]
         high = acc[:, cw:] if cw % 128 == 0 else pltpu.roll(acc, cw, 1)[:, :cw]
         first = core == 0
         w_own[cols, :] = jnp.where(first, low, high)
         w_send[cols, :] = jnp.where(first, high, low).astype(jnp.bfloat16)
-        return carry
-
-    lax.fori_loop(0, features // tile, w_tile, 0)
+
+    if not relay:
+        lax.fori_loop(0, features // tile, w_tile, 0)
+    all_g = jnp.concatenate([own_g] + [gbuf[r - 1] for r in range(1, chips)], axis=0)
 
     rows = features // chain
     subs = r_send.shape[0] // chain
@@ -331,6 +367,9 @@
 
     def send_sib(t, carry):
         flip = jnp.where(c < chain - c, up_index(t), t)
+        if relay:
+            span = pl.ds(pl.multiple_of(flip * step, 16), step)
+            w_store(span, mm(turned[span, :], all_g, 1, 0))
         s_copy(flip).start()
         return carry
 
@@ -454,7 +493,7 @@
     chips = nd // 2
     blocks = min(-(-WINDOW // count), chain - 1) + 1
     groups = width // HEAD_SIZE
-    heads = max(1, groups // 4)
+    heads = max(1, groups // 8)
     chunks = groups // heads
     ratio = queries.shape[2] // width
     cw = width // nd
@@ -483,6 +522,7 @@
             vm((blocks, count, width), f32), vm((blocks, count, width), f32),
             vm((count, blocks * count), f32),
             vm((chips - 1, count, features), bf), vm((chips - 1, count, 2 * cw), bf),
+            vm((features, chips * count) if chips == 4 else (16, 128), bf),
             vm((features, cw), f32), vm((features, cw), bf), vm((features, cw), bf),
             vm((pieces, rows // subs, cw), bf), vm((pieces, rows // subs, cw), bf), vm((pieces, rows // subs, cw), bf),
             dma((chunks, back, 2)), dma((chunks, back, 2)), dma((chunks, back, 2)), dma((chunks, back, 2)),

time: 102 us -> 93.1 us (0.913)
  Pallas kernels: 95.7 us -> 87.1 us
    pallas_call x1, Pallas kernels: 95.7 us -> 87.1 us  [body(): pl.pallas_call(functools.partial(kernel, cfg), out_shape=(jax.ShapeDtypeS...]
where the time goes in v3:
time: 93.1 us; the launch traced here: 92.9 us
  Pallas kernels  87.1 us (94%)
  local copies, waits for them, and re-layouts  5.05 us (5%)
    pallas_call x1, Pallas kernels, body(): pl.pallas_call(functools.partial(kernel, cfg), out_shape=(jax.ShapeDtypeS...  87.1 us
    unnamed x8, local copies, waits for them, and re-layouts  5.05 us

profile of v3, /device:TPU:0, one launch (start us, length us, event | category | flops | bytes accessed | tf_op | source)
XLA Modules:
  0.0 92.9 jit_solution(4677950369178657424)
XLA Ops:
  0.6 87.1 %shard_map.93 = (bf16[128,2048]{1,0:T(8,128)(2,1)}, bf16[128,1024]{1,0:T(8,128)(2,1)}, bf16[128,1024]{1,0:T(8,128)(2,1)}, bf16[1344,128]{1,0:T(8,128)(2,1)}) custom-call(bf16[128,5376]{1,0:T(8,128)(2,1)} %bitcast.8, bf16[128,2048]{1,0:T(8,128)(2,1)} %bitcast.9, bf16[128,1024]{1,0:T(8,128)(2,1)} %bitcast.12, bf16[128,1024]{1,0:T(8,128)(2,1)} %bitcast.13, ...), custom_call_target="tpu_custom_call" | custom-call | tf_op jit(solution)/shard_map/pallas_call | solution.py:508
  87.8 0.0 copy-start.1
  87.8 0.0 copy-start
  87.8 1.9 %copy.14 = bf16[1,128,2048]{2,1,0:T(8,128)(2,1)} copy(bf16[1,128,2048]{2,1,0:T(8,128)(2,1)} %bitcast.11) | data formatting | bytes 1048576
  89.7 1.7 %copy.15 = bf16[1,128,1024]{2,1,0:T(8,128)(2,1)} copy(bf16[1,128,1024]{2,1,0:T(8,128)(2,1)} %bitcast.15) | data formatting | bytes 524288
  91.4 0.0 copy-done.1
  91.4 0.7 copy.16
  92.1 0.0 copy-done
  92.1 0.7 copy.17
Async XLA Ops:
  87.8 3.6 %copy-start.1 = (bf16[128,1024]{1,0:T(8,128)(2,1)S(1)}, bf16[128,1024]{1,0:T(8,128)(2,1)}, u32[]{:S(2)}) copy-start(bf16[128,1024]{1,0:T(8,128)(2,1)} %get-tuple-element.10) | copy-start | bytes 786436
  87.8 4.3 %copy-start = (bf16[1344,128]{1,0:T(8,128)(2,1)S(1)}, bf16[1344,128]{1,0:T(8,128)(2,1)}, u32[]{:S(2)}) copy-start(bf16[1344,128]{1,0:T(8,128)(2,1)} %get-tuple-element.19) | copy-start | bytes 1032196
